TPU v7x, 32 devices: a whole 2x2x4 slice. The times are simulated.
32 devices in a mesh: gz: 16 (over z, x, core), gy: 2 (over y).
Axes of the slice: x: 2, y: 2, z: 4, core: 2. Of those that a mesh axis runs over, the one named last changes fastest.
Arguments:
- spread_weights: float32 [64, 32768], P(None, ('gz', 'gy')), may hold values from -6 to 6
- spread_base: int32 [3, 32768], P(None, ('gz', 'gy')), may hold values from 0 to 383, as said below
- qm_base: int32 [3, 4096], P(None, ('gz', 'gy')), may hold values from 0 to 383, as said below
- qm_frac: float32 [3, 4096], P(None, ('gz', 'gy')), may hold values from 0 to 1
- qm_charge: float32 [4096], P(('gz', 'gy')), may hold values from -3 to 3
Outputs:
- qm_forces: float32 [3, 4096], P(None, ('gz', 'gy'))
Inputs may be any that keep to these rules, and one draw needn't show every extreme that they name: For point charge j let d = j // 1024, p = d // 2 and q = d % 2; then spread_base[0, j] lies in [p * 24, (p + 1) * 24) and spread_base[1, j] in [q * 192, (q + 1) * 192); spread_base[2, j] is any cell. For quantum-region atom i let d = i // 128, p = d // 2 and q = d % 2; then qm_base[0, i] lies in [p * 24, (p + 1) * 24) and qm_base[1, i] in [q * 192, (q + 1) * 192); qm_base[2, i] is any cell.
All inputs are finite; a program needn't handle non-finite values.
Results may differ from a plain program's by a relative error of at most 0.0003.
Values sent between devices are 32-bit elements; how exact they have to be, the bound alone decides.
A program may use at most 256 MiB of HBM per device.

v0:
```python
import math

import jax
import jax.numpy as jnp
from jax import lax
from jax.sharding import PartitionSpec as P

GRID = 384
ORDER = 4


SPLITTING = 0.8
HIGHEST = lax.Precision.HIGHEST


def passed_along(block, axis, distance):
    devices = range(lax.axis_size(axis))
    route = [((i - distance) % len(devices), i) for i in devices]
    return lax.ppermute(block, axis, route)


def moduli(index, points):
    signed = jnp.where(index < points // 2, index, index - points).astype(jnp.float32) / points
    spline = 2.0 / 3.0 + jnp.cos(2.0 * math.pi / points * index.astype(jnp.float32)) / 3.0
    return (signed * signed, 1.0 / (spline * spline), index == points // 2)


def influence(first, second, third, points):
    sq_one, mod_one, edge_one = moduli(first, points)
    sq_two, mod_two, edge_two = moduli(second, points)
    sq_three, mod_three, edge_three = moduli(third, points)
    total = sq_one + sq_two + sq_three
    safe = jnp.where(total > 0.0, total, 1.0)
    value = (
        mod_one
        * mod_two
        * mod_three
        * jnp.exp(-(math.pi * math.pi / (SPLITTING * SPLITTING)) * total)
        / (math.pi * safe)
    )
    keep = (total > 0.0) & jnp.logical_not(edge_one | edge_two | edge_three)
    return jnp.where(keep, value, 0.0)


def spline_weights(frac):
    remain = 1.0 - frac
    square = frac * frac
    cubed = square * frac
    values = jnp.stack(
        [
            remain * remain * remain / 6.0,
            (3.0 * cubed - 6.0 * square + 4.0) / 6.0,
            (-3.0 * cubed + 3.0 * square + 3.0 * frac + 1.0) / 6.0,
            cubed / 6.0,
        ]
    )
    slopes = jnp.stack(
        [
            -0.5 * remain * remain,
            (3.0 * square - 4.0 * frac) / 2.0,
            (-3.0 * square + 2.0 * frac + 1.0) / 2.0,
            0.5 * square,
        ]
    )
    return (values, slopes)


def angle_tables(rows_in, cols_in, points):
    product = rows_in[:, None] * cols_in[None, :] % points
    angle = 2.0 * math.pi / points * product.astype(jnp.float32)
    return (jnp.cos(angle), jnp.sin(angle))


def transform(real_part, imag_part, form, cosine, sine, sign):
    first = jnp.einsum(form, real_part, cosine, precision=HIGHEST)
    second = jnp.einsum(form, imag_part, sine, precision=HIGHEST)
    third = jnp.einsum(form, imag_part, cosine, precision=HIGHEST)
    fourth = jnp.einsum(form, real_part, sine, precision=HIGHEST)
    return (first - sign * second, third + sign * fourth)


def spread_grid(spread_weights, spread_base, z_first, y_first, z_extent, y_extent, points):
    count = spread_weights.shape[1]
    weights = spread_weights.reshape(ORDER, ORDER, ORDER, count)
    shifts = jnp.arange(ORDER, dtype=jnp.int32)
    local_z = spread_base[0] - z_first
    local_y = spread_base[1] - y_first
    plane_hits = (
        jnp.arange(z_extent, dtype=jnp.int32)[None, :, None]
        == local_z[None, None, :] + shifts[:, None, None]
    ).astype(jnp.float32)
    row_hits = (
        jnp.arange(y_extent, dtype=jnp.int32)[None, :, None]
        == local_y[None, None, :] + shifts[:, None, None]
    ).astype(jnp.float32)
    column_cells = (spread_base[2][None, :] + shifts[:, None]) % points
    column_hits = (
        jnp.arange(points, dtype=jnp.int32)[None, None, :] == column_cells[:, :, None]
    ).astype(jnp.float32)
    by_plane = jnp.sum(plane_hits[:, None, :, None, :] * weights[:, :, None, :, :], axis=0)
    placed = jnp.sum(by_plane[:, :, None, :, :] * row_hits[:, None, :, None, :], axis=0)
    charge = jnp.dot(
        placed.reshape(z_extent * y_extent, ORDER * count),
        column_hits.reshape(ORDER * count, points),
        precision=HIGHEST,
        preferred_element_type=jnp.float32,
    )
    return charge.reshape(z_extent, y_extent, points)


def line_tables(cells, values, slopes, extent):
    hits = (jnp.arange(extent, dtype=jnp.int32)[None, :, None] == cells[:, None, :]).astype(
        jnp.float32
    )
    return (jnp.sum(hits * values[:, None, :], axis=0), jnp.sum(hits * slopes[:, None, :], axis=0))


def interpolate(potential, qm_base, qm_frac, qm_charge, z_first, y_first):
    z_extent, y_extent, points = potential.shape
    count = qm_charge.shape[0]
    shifts = jnp.arange(ORDER, dtype=jnp.int32)[:, None]
    w_z, d_z = spline_weights(qm_frac[0])
    w_y, d_y = spline_weights(qm_frac[1])
    w_x, d_x = spline_weights(qm_frac[2])
    plane_w, plane_d = line_tables(qm_base[0][None, :] - z_first + shifts, w_z, d_z, z_extent)
    row_w, row_d = line_tables(qm_base[1][None, :] - y_first + shifts, w_y, d_y, y_extent)
    column_w, column_d = line_tables((qm_base[2][None, :] + shifts) % points, w_x, d_x, points)
    along_x = jnp.dot(
        potential.reshape(z_extent * y_extent, points),
        jnp.concatenate([column_w, column_d], axis=1),
        precision=HIGHEST,
        preferred_element_type=jnp.float32,
    ).reshape(z_extent, y_extent, 2, count)
    plain = along_x[:, :, 0, :]
    sloped = along_x[:, :, 1, :]
    force_z = jnp.sum(plain * plane_d[:, None, :] * row_w[None, :, :], axis=(0, 1))
    force_y = jnp.sum(plain * plane_w[:, None, :] * row_d[None, :, :], axis=(0, 1))
    force_x = jnp.sum(sloped * plane_w[:, None, :] * row_w[None, :, :], axis=(0, 1))
    return jnp.stack([-qm_charge * force_z, -qm_charge * force_y, -qm_charge * force_x])


def shards(spread_weights, spread_base, qm_base, qm_frac, qm_charge):
    points = GRID
    margin = ORDER - 1
    count_z = lax.axis_size("gz")
    count_y = lax.axis_size("gy")
    z_local = points // count_z
    y_local = points // count_y
    z_extent = z_local + margin
    y_extent = y_local + margin
    z_first = lax.axis_index("gz") * z_local
    y_first = lax.axis_index("gy") * y_local
    charge = spread_grid(spread_weights, spread_base, z_first, y_first, z_extent, y_extent, points)
    spill_rows = passed_along(charge[:, y_local:, :], "gy", 1)
    charge = charge[:, :y_local, :].at[:, :margin, :].add(spill_rows)
    spill_planes = passed_along(charge[z_local:], "gz", 1)
    charge = charge[:z_local].at[:margin].add(spill_planes)
    kx_count = points // 2
    kx_weight = jnp.where(jnp.arange(kx_count, dtype=jnp.int32) == 0, 1.0, 2.0).astype(jnp.float32)
    positions = jnp.arange(points, dtype=jnp.int32)
    cos_x, sin_x = angle_tables(positions, jnp.arange(kx_count, dtype=jnp.int32), points)
    real_x = jnp.einsum("zyx,xk->kyz", charge, cos_x, precision=HIGHEST)
    imag_x = -jnp.einsum("zyx,xk->kyz", charge, sin_x, precision=HIGHEST)
    packed = jnp.stack([real_x, imag_x]).reshape(2, kx_count, y_local * z_local)
    moved = lax.all_to_all(packed, "gy", split_axis=1, concat_axis=2, tiled=True)
    kx_local = kx_count // count_y
    lines = moved.reshape(2, kx_local, count_y, y_local, z_local)
    lines = lines.reshape(2, kx_local, points, z_local)
    cos_full, sin_full = angle_tables(positions, positions, points)
    real_y, imag_y = transform(lines[0], lines[1], "xyz,yk->kzx", cos_full, sin_full, -1.0)
    packed = jnp.stack([real_y, imag_y]).reshape(2, points, z_local * kx_local)
    moved = lax.all_to_all(packed, "gz", split_axis=1, concat_axis=2, tiled=True)
    ky_local = points // count_z
    lines = moved.reshape(2, ky_local, count_z, z_local, kx_local)
    lines = lines.reshape(2, ky_local, points, kx_local)
    real_z, imag_z = transform(lines[0], lines[1], "yzx,zk->yxk", cos_full, sin_full, -1.0)
    ky_index = lax.axis_index("gz") * ky_local + jnp.arange(ky_local, dtype=jnp.int32)
    kx_index = lax.axis_index("gy") * kx_local + jnp.arange(kx_local, dtype=jnp.int32)
    green = influence(
        positions[None, None, :], ky_index[:, None, None], kx_index[None, :, None], points
    )
    real_z = real_z * green
    imag_z = imag_z * green
    z_rows = (
        (
            jnp.arange(count_z, dtype=jnp.int32)[:, None] * z_local
            + jnp.arange(z_local, dtype=jnp.int32)[None, :]
        )
        % points
    ).reshape(-1)
    cos_z, sin_z = angle_tables(positions, z_rows, points)
    back_real, back_imag = transform(real_z, imag_z, "yxk,kp->pyx", cos_z, sin_z, 1.0)
    packed = jnp.stack([back_real, back_imag]).reshape(2, count_z * z_local, ky_local * kx_local)
    moved = lax.all_to_all(packed, "gz", split_axis=1, concat_axis=2, tiled=True).reshape(
        2, z_local, points, kx_local
    )
    y_rows = (
        (
            jnp.arange(count_y, dtype=jnp.int32)[:, None] * y_local
            + jnp.arange(y_local, dtype=jnp.int32)[None, :]
        )
        % points
    ).reshape(-1)
    cos_y, sin_y = angle_tables(positions, y_rows, points)
    back_real, back_imag = transform(moved[0], moved[1], "zkx,kp->pxz", cos_y, sin_y, 1.0)
    packed = jnp.stack([back_real, back_imag]).reshape(2, count_y * y_local, kx_local * z_local)
    moved = lax.all_to_all(packed, "gy", split_axis=1, concat_axis=2, tiled=True).reshape(
        2, y_local, kx_count, z_local
    )
    scale = 1.0 / float(points * points * points)
    potential = (
        jnp.einsum("ykz,xk->zyx", moved[0], cos_x * kx_weight[None, :], precision=HIGHEST)
        - jnp.einsum("ykz,xk->zyx", moved[1], sin_x * kx_weight[None, :], precision=HIGHEST)
    ) * scale
    rim_rows = passed_along(potential[:, :margin, :], "gy", -1)
    potential = jnp.concatenate([potential, rim_rows], axis=1)
    rim_planes = passed_along(potential[:margin], "gz", -1)
    potential = jnp.concatenate([potential, rim_planes], axis=0)
    return interpolate(potential, qm_base, qm_frac, qm_charge, z_first, y_first)


def solution(mesh):
    in_specs = (
        P(None, ("gz", "gy")),
        P(None, ("gz", "gy")),
        P(None, ("gz", "gy")),
        P(None, ("gz", "gy")),
        P(("gz", "gy")),
    )
    out_specs = P(None, ("gz", "gy"))
    return jax.shard_map(shards, mesh=mesh, in_specs=in_specs, out_specs=out_specs, check_vma=False)
```

profile of v0, /device:TPU:0, one launch (start us, length us, event | category | flops | bytes accessed | tf_op | source)
XLA Modules:
  0.0 1281.5 jit_solution(2450267871987228641)
XLA Ops:
  7.1 158.1 %multiply_reduce_fusion = f32[27,195,4,1024]{3,2,1,0:T(4,128)} fusion(f32[4,195,1024]{2,1,0:T(8,128)S(1)} %fusion.18, f32[4,27,4,1024]{3,2,1,0:T(4,128)S(1)} %multiply_reduce_fusion.1), kind=kLoop, calls=%fused_computation | loop fusion | flops 150958080 | bytes 91226112 | tf_op jit(solution)/shard_map/reduce_sum | solution.py:101
  165.2 75.9 %dot_general.72 = f32[27,195,4096]{2,1,0:T(8,128)} reshape(f32[27,195,4,1024]{3,2,1,0:T(4,128)} %multiply_reduce_fusion) | data formatting | bytes 172523520 | tf_op jit(solution)/shard_map/dot_general | solution.py:102
  242.2 73.9 %fusion.6 = f32[27,195,384]{2,1,0:T(8,128)S(1)} fusion(f32[27,195,4096]{2,1,0:T(8,128)} %dot_general.72, pred[4096,384,1]{1,0,2:T(32,128)(4,1)S(1)} %fusion.280), kind=kOutput, calls=%fused_computation.18 | convolution fusion | flops 99373547520 | bytes 95921664 | tf_op jit(solution)/shard_map/dot_general | solution.py:102
  332.1 11.5 collective-permute-done.1
  344.8 9.8 convolution_bitcast_fusion
  374.1 11.4 copy.108
  385.5 80.2 %all_to_all.60 = f32[2,192,4608]{2,0,1:T(2,128)S(1)} all-to-all(f32[2,192,4608]{2,0,1:T(2,128)} %copy.108), channel_id=1, replica_groups=mesh['gz'=16,'gy'=2] {'gy'}, dimensions={1} | all-to-all | bytes 14155776 | tf_op jit(solution)/shard_map/all_to_all | solution.py:165
  476.6 10.3 fusion.44
  498.3 13.8 %fusion.42 = f32[384,96,24]{0,1,2:T(8,128)} fusion(f32[96,384,24]{1,0,2:T(8,128)} %copy.113), kind=kOutput, calls=%fused_computation.74 | convolution fusion | flops 4078190592 | bytes 7077888 | tf_op jit(solution)/shard_map/xyz,yk->kzx/dot_general | solution.py:77
  512.1 10.8 multiply_subtract_fusion
  531.8 14.2 %multiply_add_fusion = f32[384,96,24]{0,1,2:T(8,128)} fusion(f32[384,96,24]{0,1,2:T(8,128)} %fusion.42, f32[96,384,24]{1,0,2:T(8,128)S(1)} %copy.111), kind=kOutput, calls=%fused_computation.34 | convolution fusion | flops 4079960064 | bytes 10616832 | tf_op jit(solution)/shard_map/xyz,yk->kzx/dot_general | solution.py:78
  555.1 11.2 pad_maximum_fusion.1
  574.6 124.7 %all-to-all-done.1 = f32[2,384,2304]{2,0,1:T(2,128)} async-done(((f32[2,384,2304]{2,0,1:T(2,128)}), f32[2,384,2304]{2,0,1:T(2,128)}, u32[]{:S(2)}, u32[]{:S(2)}) %all-to-all-start.1) | async-done | bytes 7077920 | tf_op jit(solution)/shard_map/all_to_all | solution.py:172
  712.5 15.8 %fusion.40 = f32[24,96,384]{2,1,0:T(8,128)} fusion(f32[24,384,96]{2,1,0:T(8,128)} %squeeze.37), kind=kOutput, calls=%fused_computation.72 | convolution fusion | flops 4078190592 | bytes 7077888 | tf_op jit(solution)/shard_map/yzx,zk->yxk/dot_general | solution.py:75
  737.6 15.0 %fusion.38 = f32[24,96,384]{2,1,0:T(8,128)S(1)} fusion(f32[24,384,96]{2,1,0:T(8,128)} %squeeze.38), kind=kOutput, calls=%fused_computation.70 | convolution fusion | flops 4078190592 | bytes 7077888 | tf_op jit(solution)/shard_map/yzx,zk->yxk/dot_general | solution.py:77
  752.6 14.8 %subtract_multiply_fusion = f32[24,96,384]{2,1,0:T(8,128)S(1)} fusion(f32[24,96,384]{2,1,0:T(8,128)S(1)} %copy-done.9, f32[24,384,96]{2,1,0:T(8,128)} %squeeze.38, f32[96]{0:T(128)S(1)} %copy-done.41, f32[24,384]{1,0:T(8,128)S(1)} %copy-done.11, pred[96]{0:T(512)(128)(4,1)S(1)} %copy-done.42, pred[24,384]{1,0:T(8,128)(4,1)S(1)} %broadcast_or_fusion, ...), kind=kOutput, calls=%fused_computation.33 | convolution fusion | flops 4091461632 | bytes 10700640 | tf_op jit(solution)/shard_map/yzx,zk->yxk/dot_general | solution.py:76
  767.5 12.5 add_multiply_fusion.1
  789.2 10.7 fusion.46
  799.9 10.7 convolution_subtract_fusion
  819.5 13.8 %convolution_add_fusion = f32[384,24,96]{0,2,1:T(8,128)} fusion(f32[384,24,96]{0,2,1:T(8,128)} %fusion.46, f32[24,96,384]{2,1,0:T(8,128)S(1)} %subtract_multiply_fusion, s32[384]{0:T(512)S(1)} %add_select_fusion.7), kind=kOutput, calls=%fused_computation.47 | convolution fusion | flops 4079075328 | bytes 10618368 | tf_op jit(solution)/shard_map/yxk,kp->pyx/dot_general | solution.py:78
  842.6 11.2 pad_maximum_fusion.2
  853.9 31.3 %all-to-all-start.2 = ((f32[2,384,2304]{2,0,1:T(2,128)}), f32[2,384,2304]{2,0,1:T(2,128)}, u32[]{:S(2)}, u32[]{:S(2)}) async-start(f32[2,384,2304]{2,0,1:T(2,128)} %pad_maximum_fusion.2), calls=%async_computation.2 | async-start | bytes 14155776 | tf_op jit(solution)/shard_map/all_to_all | solution.py:194
  885.3 127.6 %all-to-all-done.2 = f32[2,384,2304]{2,0,1:T(2,128)} async-done(((f32[2,384,2304]{2,0,1:T(2,128)}), f32[2,384,2304]{2,0,1:T(2,128)}, u32[]{:S(2)}, u32[]{:S(2)}) %all-to-all-start.2) | async-done | bytes 7077920 | tf_op jit(solution)/shard_map/all_to_all | solution.py:194
  1028.6 10.3 fusion.80
  1038.8 10.4 fusion.74
  1086.2 12.3 copy.136
  1107.2 77.8 %all-to-all-done.3 = f32[2,384,2304]{2,0,1:T(2,128)} async-done(((f32[2,384,2304]{2,0,1:T(2,128)}), f32[2,384,2304]{2,0,1:T(2,128)}, u32[]{:S(2)}, u32[]{:S(2)}) %all-to-all-start.3) | async-done | bytes 7077920 | tf_op jit(solution)/shard_map/all_to_all | solution.py:207
  1200.0 12.9 %fusion.8 = f32[384,192,24]{0,1,2:T(8,128)S(1)} fusion(f32[192,192,24]{0,2,1:T(8,128)} %bitcast.186, f32[192]{0:T(256)S(1)} %compare_select_fusion.3), kind=kOutput, calls=%fused_computation.19 | convolution fusion | flops 4077600768 | bytes 10617600 | tf_op jit(solution)/shard_map/ykz,xk->zyx/dot_general | solution.py:213
  1213.0 10.8 multiply_bitcast_fusion
  1229.9 27.0 %collective-permute-start.3 = (f32[3,195,384]{2,1,0:T(8,128)S(1)}, f32[3,195,384]{2,1,0:T(8,128)S(1)}, u32[]{:S(2)}, u32[]{:S(2)}) collective-permute-start(f32[3,195,384]{2,1,0:T(8,128)S(1)} %pad_maximum_fusion.4), channel_id=1, source_target_pairs={{2,0},{4,2},{6,4},{8,6},{10,8},{12,10},{14,12},{16,14},{18,16},{20... | collective-permute-start | bytes 2695688 | tf_op jit(solution)/shard_map/ppermute | solution.py:19
  1258.1 9.8 collective-permute-done.3
  1267.9 11.8 fusion
  (193 shorter events, 227.9 us)
Async XLA Ops:
  165.2 75.9 %copy-start.12 = (s32[1,1024]{1,0:T(1,128)S(1)}, s32[1,1024]{1,0:T(1,128)}, u32[]{:S(2)}) copy-start(s32[1,1024]{1,0:T(1,128)} %get-tuple-element.46) | copy-start | bytes 12292
  316.1 7.3 collective-permute-start
  328.3 15.2 %collective-permute-start.1 = (f32[3,192,384]{2,1,0:T(8,128)S(1)}, f32[3,192,384]{2,1,0:T(8,128)S(1)}, u32[]{:S(2)}, u32[]{:S(2)}) collective-permute-start(f32[3,192,384]{2,1,0:T(8,128)S(1)} %slice.168), channel_id=1, source_target_pairs={{30,0},{0,2},{2,4},{4,6},{6,8},{8,10},{10,12},{12,14},{14,16},{16,... | collective-permute-start | bytes 2654216 | tf_op jit(solution)/shard_map/ppermute | solution.py:19
  566.4 133.0 %all-to-all-start.1 = ((f32[2,384,2304]{2,0,1:T(2,128)}), f32[2,384,2304]{2,0,1:T(2,128)}, u32[]{:S(2)}, u32[]{:S(2)}) async-start(f32[2,384,2304]{2,0,1:T(2,128)} %pad_maximum_fusion.1), calls=%async_computation.1 | async-start | bytes 14155776 | tf_op jit(solution)/shard_map/all_to_all | solution.py:172
  737.5 15.1 %copy-start.9 = (f32[24,96,384]{2,1,0:T(8,128)S(1)}, f32[24,96,384]{2,1,0:T(8,128)}, u32[]{:S(2)}) copy-start(f32[24,96,384]{2,1,0:T(8,128)} %fusion.40) | copy-start | bytes 10616836
  737.5 15.1 %copy-start.10 = (f32[24,384]{1,0:T(8,128)S(1)}, f32[24,384]{1,0:T(8,128)}, u32[]{:S(2)}) copy-start(f32[24,384]{1,0:T(8,128)} %broadcast_add_fusion) | copy-start | bytes 110596
  737.5 15.1 %copy-start.11 = (f32[24,384]{1,0:T(8,128)S(1)}, f32[24,384]{1,0:T(8,128)}, u32[]{:S(2)}) copy-start(f32[24,384]{1,0:T(8,128)} %broadcast_multiply_fusion) | copy-start | bytes 110596
  737.5 15.1 %copy-start.40 = (f32[96]{0:T(128)S(1)}, f32[96]{0:T(128)}, u32[]{:S(2)}) copy-start(f32[96]{0:T(128)} %get-tuple-element.81) | copy-start | bytes 1156
  737.5 15.1 %copy-start.41 = (f32[96]{0:T(128)S(1)}, f32[96]{0:T(128)}, u32[]{:S(2)}) copy-start(f32[96]{0:T(128)} %get-tuple-element.82) | copy-start | bytes 1156
  737.5 15.1 %copy-start.42 = (pred[96]{0:T(512)(128)(4,1)S(1)}, pred[96]{0:T(512)(128)(4,1)}, u32[]{:S(2)}) copy-start(pred[96]{0:T(512)(128)(4,1)} %fusion.189) | copy-start | bytes 292
  737.5 29.9 %slice-start = ((s8[4718592]{0:T(1024)(128)(4,1)}), s8[4194304]{0:T(1024)(128)(4,1)S(1)}, s32[]{:S(2)}) async-start(s8[4718592]{0:T(1024)(128)(4,1)} %bitcast.187), calls=%async_computation.4 | async-start | bytes 8388608
  752.6 14.8 %slice-start.1 = ((s8[4718592]{0:T(1024)(128)(4,1)}), s8[524288]{0:T(1024)(128)(4,1)S(1)}, s32[]{:S(2)}) async-start(s8[4718592]{0:T(1024)(128)(4,1)} %bitcast.187), calls=%async_computation.5 | async-start | bytes 1048576
  853.9 159.0 %all-to-all-start.2 = ((f32[2,384,2304]{2,0,1:T(2,128)}), f32[2,384,2304]{2,0,1:T(2,128)}, u32[]{:S(2)}, u32[]{:S(2)}) async-start(f32[2,384,2304]{2,0,1:T(2,128)} %pad_maximum_fusion.2), calls=%async_computation.2 | async-start | bytes 14155776 | tf_op jit(solution)/shard_map/all_to_all | solution.py:194
  1098.6 86.5 %all-to-all-start.3 = ((f32[2,384,2304]{2,0,1:T(2,128)}), f32[2,384,2304]{2,0,1:T(2,128)}, u32[]{:S(2)}, u32[]{:S(2)}) async-start(f32[2,384,2304]{2,0,1:T(2,128)} %copy.136), calls=%async_computation.3 | async-start | bytes 14155776 | tf_op jit(solution)/shard_map/all_to_all | solution.py:207
  1223.9 5.9 collective-permute-start.2
  1224.1 33.2 %copy-start.16 = (f32[1,128]{1,0:T(1,128)S(1)}, f32[1,128]{1,0:T(1,128)}, u32[]{:S(2)}) copy-start(f32[1,128]{1,0:T(1,128)} %get-tuple-element.71) | copy-start | bytes 1540
  1224.1 33.2 %copy-start.22 = (f32[1,128]{1,0:T(1,128)S(1)}, f32[1,128]{1,0:T(1,128)}, u32[]{:S(2)}) copy-start(f32[1,128]{1,0:T(1,128)} %get-tuple-element.57) | copy-start | bytes 1540
  1224.1 33.2 %copy-start.23 = (f32[1,128]{1,0:T(1,128)S(1)}, f32[1,128]{1,0:T(1,128)}, u32[]{:S(2)}) copy-start(f32[1,128]{1,0:T(1,128)} %get-tuple-element.58) | copy-start | bytes 1540
  1224.1 33.2 %copy-start.24 = (f32[1,128]{1,0:T(1,128)S(1)}, f32[1,128]{1,0:T(1,128)}, u32[]{:S(2)}) copy-start(f32[1,128]{1,0:T(1,128)} %get-tuple-element.59) | copy-start | bytes 1540
  1224.1 33.2 %copy-start.25 = (f32[1,128]{1,0:T(1,128)S(1)}, f32[1,128]{1,0:T(1,128)}, u32[]{:S(2)}) copy-start(f32[1,128]{1,0:T(1,128)} %get-tuple-element.63) | copy-start | bytes 1540
  1224.1 33.2 %copy-start.26 = (f32[1,128]{1,0:T(1,128)S(1)}, f32[1,128]{1,0:T(1,128)}, u32[]{:S(2)}) copy-start(f32[1,128]{1,0:T(1,128)} %get-tuple-element.64) | copy-start | bytes 1540
  1224.1 33.2 %copy-start.27 = (f32[1,128]{1,0:T(1,128)S(1)}, f32[1,128]{1,0:T(1,128)}, u32[]{:S(2)}) copy-start(f32[1,128]{1,0:T(1,128)} %get-tuple-element.65) | copy-start | bytes 1540
  1224.1 33.2 %copy-start.28 = (f32[1,128]{1,0:T(1,128)S(1)}, f32[1,128]{1,0:T(1,128)}, u32[]{:S(2)}) copy-start(f32[1,128]{1,0:T(1,128)} %get-tuple-element.66) | copy-start | bytes 1540
  1224.1 33.2 %copy-start.14 = (f32[1,128]{1,0:T(1,128)S(1)}, f32[1,128]{1,0:T(1,128)}, u32[]{:S(2)}) copy-start(f32[1,128]{1,0:T(1,128)} %get-tuple-element.73) | copy-start | bytes 1540
  1224.1 33.2 %copy-start.15 = (f32[1,128]{1,0:T(1,128)S(1)}, f32[1,128]{1,0:T(1,128)}, u32[]{:S(2)}) copy-start(f32[1,128]{1,0:T(1,128)} %get-tuple-element.75) | copy-start | bytes 1540
  1224.2 33.2 %copy-start.17 = (f32[1,128]{1,0:T(1,128)S(1)}, f32[1,128]{1,0:T(1,128)}, u32[]{:S(2)}) copy-start(f32[1,128]{1,0:T(1,128)} %get-tuple-element.49) | copy-start | bytes 1540
  1224.2 33.2 %copy-start.18 = (f32[1,128]{1,0:T(1,128)S(1)}, f32[1,128]{1,0:T(1,128)}, u32[]{:S(2)}) copy-start(f32[1,128]{1,0:T(1,128)} %get-tuple-element.60) | copy-start | bytes 1540
  1224.2 33.2 %copy-start.19 = (f32[1,128]{1,0:T(1,128)S(1)}, f32[1,128]{1,0:T(1,128)}, u32[]{:S(2)}) copy-start(f32[1,128]{1,0:T(1,128)} %get-tuple-element.61) | copy-start | bytes 1540
  1224.2 33.2 %copy-start.20 = (f32[1,128]{1,0:T(1,128)S(1)}, f32[1,128]{1,0:T(1,128)}, u32[]{:S(2)}) copy-start(f32[1,128]{1,0:T(1,128)} %get-tuple-element.62) | copy-start | bytes 1540
  1224.2 33.2 %copy-start.21 = (f32[1,128]{1,0:T(1,128)S(1)}, f32[1,128]{1,0:T(1,128)}, u32[]{:S(2)}) copy-start(f32[1,128]{1,0:T(1,128)} %get-tuple-element.67) | copy-start | bytes 1540
  1224.2 33.3 %copy-start.37 = (s32[128]{0:T(128)S(1)}, s32[128]{0:T(128)}, u32[]{:S(2)}) copy-start(s32[128]{0:T(128)} %get-tuple-element.68) | copy-start | bytes 1540
  1229.9 38.0 %collective-permute-start.3 = (f32[3,195,384]{2,1,0:T(8,128)S(1)}, f32[3,195,384]{2,1,0:T(8,128)S(1)}, u32[]{:S(2)}, u32[]{:S(2)}) collective-permute-start(f32[3,195,384]{2,1,0:T(8,128)S(1)} %pad_maximum_fusion.4), channel_id=1, source_target_pairs={{2,0},{4,2},{6,4},{8,6},{10,8},{12,10},{14,12},{16,14},{18,16},{20... | collective-permute-start | bytes 2695688 | tf_op jit(solution)/shard_map/ppermute | solution.py:19
  (20 other events, 190.4 us)
where the time goes:
time: 1290 us; the launch traced here: 1280 us
  waiting for transfers between devices  357 us (28%)
  matrix products  320 us (25%)
  local copies, waits for them, and re-layouts  245 us (19%)
  other arithmetic  205 us (16%)
  blocking collectives  80.2 us (6%)
  starting transfers between devices  73.5 us (6%)
    all_to_all x2, waiting for transfers between devices, shards(): lax.all_to_all(packed, 'gz', split_axis=1, concat_axis=2, tiled=True)  252 us
    reduce_sum x1, other arithmetic, spread_grid(): jnp.sum(by_plane[:, :, None, :, :] * row_hits[:, None, :, None, :], axis=0)  158 us
    all_to_all x1, blocking collectives, shards(): lax.all_to_all(packed, 'gy', split_axis=1, concat_axis=2, tiled=True)  80.2 us
    all_to_all x1, waiting for transfers between devices, shards(): lax.all_to_all(packed, 'gy', split_axis=1, concat_axis=2, tiled=True)  77.8 us
    dot_general x1, local copies, waits for them, and re-layouts, spread_grid(): jnp.dot(placed.reshape(z_extent * y_extent, ORDER * count), column_hits.r...  75.9 us
    dot_general x1, matrix products, spread_grid(): jnp.dot(placed.reshape(z_extent * y_extent, ORDER * count), column_hits.r...  73.9 us
    dot_general x3, matrix products, transform(): fourth = jnp.einsum(form, real_part, sine, precision=HIGHEST)  40.4 us
    unnamed x4, matrix products  39.6 us
  transfers between devices with their start and end apart: 7, of which 7 were waited for; matrix products, arithmetic and copies ran while one was open for 1% of the time, Pallas kernels for 0%

commit v1 on v0

v1 whole, which is shorter than its diff:
```python
import math

import jax
import jax.numpy as jnp
from jax import lax
from jax.experimental import pallas as pl
from jax.experimental.pallas import tpu as pltpu
from jax.sharding import PartitionSpec as P

GRID = 384
ORDER = 4


SPLITTING = 0.8
HIGHEST = lax.Precision.HIGHEST
HIGH = lax.Precision.HIGH
GROUP = 64


def moduli(index, points):
    signed = jnp.where(index < points // 2, index, index - points).astype(jnp.float32) / points
    spline = 2.0 / 3.0 + jnp.cos(2.0 * math.pi / points * index.astype(jnp.float32)) / 3.0
    return (signed * signed, 1.0 / (spline * spline), index == points // 2)


def influence(first, second, third, points):
    sq_one, mod_one, edge_one = moduli(first, points)
    sq_two, mod_two, edge_two = moduli(second, points)
    sq_three, mod_three, edge_three = moduli(third, points)
    total = sq_one + sq_two + sq_three
    safe = jnp.where(total > 0.0, total, 1.0)
    value = (
        mod_one
        * mod_two
        * mod_three
        * jnp.exp(-(math.pi * math.pi / (SPLITTING * SPLITTING)) * total)
        / (math.pi * safe)
    )
    keep = (total > 0.0) & jnp.logical_not(edge_one | edge_two | edge_three)
    return jnp.where(keep, value, 0.0)


def spline_weights(frac):
    remain = 1.0 - frac
    square = frac * frac
    cubed = square * frac
    values = jnp.stack(
        [
            remain * remain * remain / 6.0,
            (3.0 * cubed - 6.0 * square + 4.0) / 6.0,
            (-3.0 * cubed + 3.0 * square + 3.0 * frac + 1.0) / 6.0,
            cubed / 6.0,
        ]
    )
    slopes = jnp.stack(
        [
            -0.5 * remain * remain,
            (3.0 * square - 4.0 * frac) / 2.0,
            (-3.0 * square + 2.0 * frac + 1.0) / 2.0,
            0.5 * square,
        ]
    )
    return (values, slopes)


def angle_tables(rows_in, cols_in, points):
    product = rows_in[:, None] * cols_in[None, :] % points
    angle = 2.0 * math.pi / points * product.astype(jnp.float32)
    return (jnp.cos(angle), jnp.sin(angle))


def line_tables(cells, values, slopes, extent):
    hits = (jnp.arange(extent, dtype=jnp.int32)[None, :, None] == cells[:, None, :]).astype(
        jnp.float32
    )
    return (jnp.sum(hits * values[:, None, :], axis=0), jnp.sum(hits * slopes[:, None, :], axis=0))


def spread_kernel(first_ref, count_ref, weights_ref, z_ref, y_ref, waves_ref, out_ref):
    half = pl.program_id(0)
    group = pl.program_id(1)

    @pl.when(group == 0)
    def _():
        out_ref[...] = jnp.zeros_like(out_ref)

    rows = out_ref.shape[1]
    weights = weights_ref[...]
    z_cell = z_ref[...]
    y_cell = y_ref[...]
    waves = waves_ref[...]
    high = waves.astype(jnp.bfloat16)
    low = (waves - high.astype(jnp.float32)).astype(jnp.bfloat16)
    first = first_ref[half, group]
    row_offset = lax.broadcasted_iota(jnp.int32, (rows, weights.shape[1]), 0) - y_cell

    def plane(step, carry):
        z = first + step
        offset = z - z_cell
        chosen = jnp.zeros((ORDER, weights.shape[1]), jnp.float32)
        for a in range(ORDER):
            chosen = jnp.where(offset == a, weights[a * ORDER : (a + 1) * ORDER], chosen)
        placed = jnp.zeros((rows, weights.shape[1]), jnp.float32)
        for b in range(ORDER):
            placed = jnp.where(row_offset == b, chosen[b : b + 1], placed)
        top = placed.astype(jnp.bfloat16)
        rest = (placed - top.astype(jnp.float32)).astype(jnp.bfloat16)
        total = jnp.dot(top, high, preferred_element_type=jnp.float32)
        total += jnp.dot(rest, high, preferred_element_type=jnp.float32)
        total += jnp.dot(top, low, preferred_element_type=jnp.float32)
        out_ref[z] += total
        return carry

    lax.fori_loop(0, count_ref[half, group], plane, 0)


def sort_by_plane(table, local_z):
    count = local_z.shape[0]
    order = jnp.arange(count, dtype=jnp.int32)
    before = (local_z[:, None] < local_z[None, :]) | (
        (local_z[:, None] == local_z[None, :]) & (order[:, None] < order[None, :])
    )
    rank = jnp.sum(before.astype(jnp.int32), axis=0)
    moves = (rank[:, None] == order[None, :]).astype(jnp.float32)
    return jnp.dot(table, moves, precision=HIGHEST)


def phases(cells, index, points):
    angle = (2.0 * math.pi / points) * (cells[..., None] * index % points).astype(jnp.float32)
    return (jnp.cos(angle), jnp.sin(angle))


def spread_lines(spread_weights, spread_base, z_first, y_first, z_extent, y_local, kx_index, points):
    count = spread_weights.shape[1]
    halves = lax.axis_size("gy")
    local = jnp.stack([spread_base[0] - z_first, spread_base[1] - y_first, spread_base[2]])
    table = jnp.concatenate([spread_weights, local.astype(jnp.float32)], axis=0)
    table = sort_by_plane(table, local[0])
    table = lax.all_gather(table, "gy")
    groups = count // GROUP
    width = ORDER * GROUP
    weights = table[:, : ORDER**3].reshape(halves, ORDER * ORDER, ORDER, groups, GROUP)
    weights = weights.transpose(0, 3, 1, 2, 4).reshape(halves, groups, ORDER * ORDER, width)
    cells = jnp.round(table[:, ORDER**3 :]).astype(jnp.int32).reshape(halves, 3, groups, GROUP)
    z_cell, y_cell, x_cell = cells[:, 0], cells[:, 1], cells[:, 2]
    first = jnp.min(z_cell, axis=-1)
    planes = jnp.max(z_cell, axis=-1) - first + ORDER
    z_wide = jnp.tile(z_cell, (1, 1, ORDER))[:, :, None, :]
    y_wide = jnp.tile(y_cell, (1, 1, ORDER))[:, :, None, :]
    cosine, sine = phases(x_cell, kx_index, points)
    step_cos, step_sin = phases(jnp.arange(ORDER, dtype=jnp.int32), kx_index, points)
    step_cos, step_sin = step_cos[:, None, :], step_sin[:, None, :]
    cosine, sine = cosine[:, :, None], sine[:, :, None]
    waves = jnp.concatenate(
        [cosine * step_cos - sine * step_sin, -(sine * step_cos + cosine * step_sin)], axis=-1
    ).reshape(halves, groups, width, -1)
    rows = -(-(y_local + ORDER - 1) // 8) * 8
    lanes = waves.shape[-1]
    per_group = lambda q, g, *_: (q, g, 0, 0)
    lines = pl.pallas_call(
        spread_kernel,
        grid_spec=pltpu.PrefetchScalarGridSpec(
            num_scalar_prefetch=2,
            grid=(halves, groups),
            in_specs=[
                pl.BlockSpec((None, None, ORDER * ORDER, width), per_group),
                pl.BlockSpec((None, None, 1, width), per_group),
                pl.BlockSpec((None, None, 1, width), per_group),
                pl.BlockSpec((None, None, width, lanes), per_group),
            ],
            out_specs=pl.BlockSpec((z_extent, None, rows, lanes), lambda q, g, *_: (0, q, 0, 0)),
        ),
        out_shape=jax.ShapeDtypeStruct((z_extent, halves, rows, lanes), jnp.float32),
        compiler_params=pltpu.CompilerParams(dimension_semantics=("arbitrary", "arbitrary")),
    )(first, planes, weights, z_wide, y_wide, waves)
    return lines, rows


def line_waves(cell, values, slopes, index, points):
    cosine, sine = phases(cell, index, points)
    step_cos, step_sin = phases(jnp.arange(ORDER, dtype=jnp.int32), index, points)
    found = []
    for table in (values, slopes):
        real = sum(table[c][..., None] * step_cos[c] for c in range(ORDER))
        imag = sum(table[c][..., None] * step_sin[c] for c in range(ORDER))
        found.append((cosine * real - sine * imag, cosine * imag + sine * real))
    return found


def slab_forces(lines, base, frac, z_first, y_index, x_index, points):
    z_extent, ky_local, _, kx_local = lines.shape
    shifts = jnp.arange(ORDER, dtype=jnp.int32)[:, None]
    w_z, d_z = spline_weights(frac[0])
    w_y, d_y = spline_weights(frac[1])
    w_x, d_x = spline_weights(frac[2])
    plane_w, plane_d = line_tables(base[0][None, :] - z_first + shifts, w_z, d_z, z_extent)
    (wy_re, wy_im), (dy_re, dy_im) = line_waves(base[1], w_y, d_y, y_index, points)
    (wx_re, wx_im), (dx_re, dx_im) = line_waves(base[2], w_x, d_x, x_index, points)
    join = lambda a, b: jnp.concatenate([a, b], axis=1)
    waves = jnp.stack([join(wx_re, -wx_im), join(wx_im, wx_re), join(dx_re, -dx_im), join(dx_im, dx_re)])
    count = base.shape[1]
    along = jnp.einsum(
        "mk,nk->mn",
        lines.reshape(z_extent * ky_local, 2 * kx_local),
        waves.reshape(4 * count, 2 * kx_local),
        precision=HIGH,
    ).reshape(z_extent, ky_local, 4, count)
    wy_re, wy_im, dy_re, dy_im = wy_re.T, wy_im.T, dy_re.T, dy_im.T
    plain = jnp.sum(along[:, :, 0] * wy_re - along[:, :, 1] * wy_im, axis=1)
    tilted = jnp.sum(along[:, :, 0] * dy_re - along[:, :, 1] * dy_im, axis=1)
    sloped = jnp.sum(along[:, :, 2] * wy_re - along[:, :, 3] * wy_im, axis=1)
    return jnp.stack(
        [
            jnp.sum(plain * plane_d, axis=0),
            jnp.sum(tilted * plane_w, axis=0),
            jnp.sum(sloped * plane_w, axis=0),
        ]
    )


def shards(spread_weights, spread_base, qm_base, qm_frac, qm_charge):
    points = GRID
    margin = ORDER - 1
    count_z = lax.axis_size("gz")
    count_y = lax.axis_size("gy")
    z_local = points // count_z
    y_local = points // count_y
    z_extent = z_local + margin
    kx_count = points // 2
    kx_local = kx_count // count_y
    ky_local = points // count_z
    z_first = lax.axis_index("gz") * z_local
    y_first = lax.axis_index("gy") * y_local
    ky_index = lax.axis_index("gz") * ky_local + jnp.arange(ky_local, dtype=jnp.int32)
    kx_index = lax.axis_index("gy") * kx_local + jnp.arange(kx_local, dtype=jnp.int32)
    positions = jnp.arange(points, dtype=jnp.int32)
    all_base = lax.all_gather(qm_base, ("gz", "gy"), axis=1, tiled=True)
    all_frac = lax.all_gather(qm_frac, ("gz", "gy"), axis=1, tiled=True)

    lines, rows = spread_lines(
        spread_weights, spread_base, z_first, y_first, z_extent, y_local, kx_index, points
    )
    row_cells = (
        jnp.arange(count_y, dtype=jnp.int32)[:, None] * y_local
        + jnp.arange(rows, dtype=jnp.int32)[None, :]
    ).reshape(-1) % points
    tables = jnp.concatenate(angle_tables(positions, row_cells, points), axis=0)
    lines = lines.reshape(z_extent, count_y * rows, 2 * kx_local)
    both = jnp.einsum("yr,zrk->zyk", tables, lines, precision=HIGH)
    with_cos, with_sin = both[:, :points], both[:, points:]
    packed = jnp.stack(
        [
            with_cos[:, :, :kx_local] + with_sin[:, :, kx_local:],
            with_cos[:, :, kx_local:] - with_sin[:, :, :kx_local],
        ],
        axis=1,
    )
    packed = packed.reshape(z_extent, 2, count_z, ky_local, kx_local).transpose(2, 0, 1, 3, 4)
    packed = packed.reshape(count_z, z_extent * 2 * ky_local * kx_local)
    moved = lax.all_to_all(packed, "gz", split_axis=0, concat_axis=0, tiled=True)

    z_cells = (
        jnp.arange(count_z, dtype=jnp.int32)[:, None] * z_local
        + jnp.arange(z_extent, dtype=jnp.int32)[None, :]
    ).reshape(-1) % points
    cells = ky_local * kx_local
    moved = moved.reshape(count_z * z_extent, 2 * cells)
    tables = jnp.concatenate(angle_tables(positions, z_cells, points), axis=0)
    both = jnp.dot(tables, moved, precision=HIGH).reshape(2, points, 2, ky_local, kx_local)
    green = influence(
        positions[:, None, None], ky_index[None, :, None], kx_index[None, None, :], points
    )
    kx_weight = jnp.where(kx_index == 0, 1.0, 2.0).astype(jnp.float32)
    green = green * (kx_weight * (1.0 / float(points * points * points)))
    spectrum = jnp.stack(
        [(both[0, :, 0] + both[1, :, 1]) * green, (both[0, :, 1] - both[1, :, 0]) * green], axis=1
    ).reshape(points, 2 * cells)
    back = jnp.concatenate(angle_tables(z_cells, positions, points), axis=0)
    both = jnp.dot(back, spectrum, precision=HIGH)
    both = both.reshape(2, count_z, z_extent, 2, ky_local, kx_local)
    lines = jnp.stack(
        [both[0, :, :, 0] - both[1, :, :, 1], both[0, :, :, 1] + both[1, :, :, 0]], axis=3
    )

    def one_slab(args):
        slab, base, frac, start = args
        return slab_forces(slab, base, frac, start, ky_index, kx_index, points)

    slab_base = all_base.reshape(3, count_z, -1).transpose(1, 0, 2)
    slab_frac = all_frac.reshape(3, count_z, -1).transpose(1, 0, 2)
    starts = jnp.arange(count_z, dtype=jnp.int32) * z_local
    partial = lax.map(one_slab, (lines, slab_base, slab_frac, starts))
    forces = lax.psum_scatter(
        partial.transpose(1, 0, 2).reshape(3, -1), ("gz", "gy"), scatter_dimension=1, tiled=True
    )
    return -qm_charge * forces


def solution(mesh):
    in_specs = (
        P(None, ("gz", "gy")),
        P(None, ("gz", "gy")),
        P(None, ("gz", "gy")),
        P(None, ("gz", "gy")),
        P(("gz", "gy")),
    )
    out_specs = P(None, ("gz", "gy"))
    return jax.shard_map(shards, mesh=mesh, in_specs=in_specs, out_specs=out_specs, check_vma=False)
```

time: 1290 us -> 884 us (0.69)
  matrix products: 320 us -> 82.2 us
  waiting for transfers between devices: 357 us -> 134 us
  blocking collectives: 80.2 us -> 287 us
  local copies, waits for them, and re-layouts: 245 us -> 113 us
  starting transfers between devices: 73.5 us -> 5.95 us
  Pallas kernels: 0 us -> 55.5 us
  other arithmetic: 205 us -> 179 us
    all_to_all x3 -> x1, waiting for transfers between devices: 330 us -> 0.01 us  [shards(): lax.all_to_all(packed, 'gz', split_axis=0, concat_axis=0, tiled=True)]
    all_gather x0 -> x3, blocking collectives: none -> 287 us  [the longest x1 184 us: shards(): all_base = lax.all_gather(qm_base, ('gz', 'gy'), axis=1, tiled=True)]
    dot_general x18 -> x20, matrix products: 280 us -> 82.2 us  [the longest x1 23.1 us: shards(): both = jnp.dot(back, spectrum, precision=HIGH)]
    reduce_sum x4 -> x49, other arithmetic: 163 us -> 10.2 us  [the longest x16 8.61 us: slab_forces(): plain = jnp.sum(along[:, :, 0] * wy_re - along[:, :, 1] * wy_im, axis=1)]
    unnamed x0 -> x2, waiting for transfers between devices: none -> 134 us
    all_to_all x1 -> x0, blocking collectives: 80.2 us -> none  [shards(): lax.all_to_all(packed, 'gy', split_axis=1, concat_axis=2, tiled=True)]
    all_to_all x0 -> x1, other arithmetic: none -> 71.6 us  [shards(): lax.all_to_all(packed, 'gz', split_axis=0, concat_axis=0, tiled=True)]
    dot_general x2 -> x19, local copies, waits for them, and re-layouts: 76 us -> 17.4 us  [the longest x2 11.1 us: shards(): jnp.dot(tables, moved, precision=HIGH)]
  transfers between devices with their start and end apart: 7 -> 2, of which waited for: 7 -> 1; matrix products, arithmetic and copies ran while one was open for 1% -> 1% of each run, Pallas kernels for 0% -> 0%
where the time goes in v1:
time: 884 us; the launch traced here: 874 us
  blocking collectives  287 us (32%)
  other arithmetic  179 us (20%)
  waiting for transfers between devices  134 us (15%)
  local copies, waits for them, and re-layouts  113 us (13%)
  matrix products  82.2 us (9%)
  Pallas kernels  55.5 us (6%)
  between operations  14.2 us (2%)
    all_gather x1, blocking collectives, shards(): all_base = lax.all_gather(qm_base, ('gz', 'gy'), axis=1, tiled=True)  184 us
    unnamed x2, waiting for transfers between devices  134 us
    all_gather x1, blocking collectives, shards(): all_frac = lax.all_gather(qm_frac, ('gz', 'gy'), axis=1, tiled=True)  91.7 us
    all_to_all x1, other arithmetic, shards(): lax.all_to_all(packed, 'gz', split_axis=0, concat_axis=0, tiled=True)  71.6 us
    pallas_call x1, Pallas kernels, spread_lines(): pl.pallas_call(spread_kernel, grid_spec=pltpu.PrefetchScalarGridSpec(num_...  55.5 us
    dynamic_slice x32, local copies, waits for them, and re-layouts, shards(): partial = lax.map(one_slab, (lines, slab_base, slab_frac, starts))  28 us
    dot_general x1, matrix products, shards(): both = jnp.dot(back, spectrum, precision=HIGH)  23.1 us
    unnamed x13, local copies, waits for them, and re-layouts  22.9 us
  transfers between devices with their start and end apart: 2, of which 1 were waited for; matrix products, arithmetic and copies ran while one was open for 1% of the time, Pallas kernels for 0%

profile of v1, /device:TPU:0, one launch (start us, length us, event | category | flops | bytes accessed | tf_op | source)
XLA Modules:
  0.0 873.9 jit_solution(13381775178883817362)
XLA Ops:
  8.2 2.7 fusion.84
  10.8 10.7 %all-gather.1 = f32[2,67,1024]{2,1,0:T(8,128)S(1)} all-gather(f32[1,67,1024]{2,1,0:T(8,128)S(1)} %fusion.84), channel_id=2, replica_groups=mesh['gz'=16,'gy'=2] {'gy'}, dimensions={0}, use_global_device_ids=true | all-gather | bytes 823296 | tf_op jit(solution)/shard_map/all_gather | solution.py:139
  21.9 5.7 fusion.90
  31.5 2.6 fusion.111
  34.1 2.4 fusion.61
  36.5 5.5 pad_maximum_fusion.3.waves_ref
  42.5 55.5 %shard_map.55 = f32[27,2,200,192]{3,2,1,0:T(8,128)} custom-call(s32[2,16]{1,0:T(2,128)} %copy-done.1, s32[2,16]{1,0:T(2,128)} %subtract_add_fusion.count_ref, f32[2,16,16,256]{3,2,1,0:T(8,128)} %reshape.2142.weights_ref, s32[2,16,1,256]{3,2,1,0:T(1,128)} %tile.20.z_ref, s32[2,16,1,256]{3,2,1,0:T(1,128)} %tile.23.y_ref, ...), custom_call_target="tpu_custom_call" | custom-call | tf_op jit(solution)/shard_map/pallas_call | solution.py:160
  98.0 21.7 %convolution_bitcast_fusion = f32[27,768,192]{1,2,0:T(8,128)} fusion(f32[27,400,192]{2,1,0:T(8,128)} %bitcast.230, f32[384,400]{0,1:T(8,128)S(1)} %get-tuple-element.286, f32[384,400]{0,1:T(8,128)S(1)} %get-tuple-element.285), kind=kOutput, calls=%fused_computation.150 | convolution fusion | flops 9555456000 | bytes 25448448 | tf_op jit(solution)/shard_map/yr,zrk->zyk/dot_general | solution.py:249
  119.7 10.1 %slice_add_fusion.1 = (f32[27,384,96]{1,2,0:T(8,128)}, f32[27,384,96]{1,2,0:T(8,128)}) fusion(f32[27,768,192]{1,2,0:T(8,128)} %convolution_bitcast_fusion), kind=kLoop, calls=%fused_computation.179 | loop fusion | flops 1990656 | bytes 23887872 | tf_op jit(solution)/shard_map/add | solution.py:253
  129.8 5.9 copy.52
  135.7 5.9 copy.53
  141.6 4.9 maximum_bitcast_fusion.7
  146.5 4.9 copy.54
  151.4 17.5 %all_to_all.8 = f32[16,1,124416]{2,1,0:T(1,128)} reshape(f32[16,27,2,24,96]{4,3,2,1,0:T(8,128)} %copy.54) | data formatting | bytes 15925248 | tf_op jit(solution)/shard_map/all_to_all | solution.py:260
  168.9 5.9 all-to-all-start
  175.1 2.8 fusion.99
  179.7 2.7 fusion.103
  182.8 184.2 %all_gather.14 = s32[3,4096]{1,0:T(4,128)S(1)} all-gather(s32[3,128]{1,0:T(4,128)S(1)} %copy-done.2), channel_id=1, replica_groups=mesh['gz'=16,'gy'=2] {'gz','gy'}, dimensions={1}, use_global_device_ids=true | all-gather | bytes 50688 | tf_op jit(solution)/shard_map/all_gather | solution.py:237
  367.0 91.7 %all_gather.15 = f32[3,4096]{1,0:T(4,128)S(1)} all-gather(f32[3,128]{1,0:T(4,128)S(1)} %copy-done.3), channel_id=1, replica_groups=mesh['gz'=16,'gy'=2] {'gz','gy'}, dimensions={1}, use_global_device_ids=true | all-gather | bytes 50688 | tf_op jit(solution)/shard_map/all_gather | solution.py:238
  459.2 71.6 %reduce.2 = f32[16,124416]{1,0:T(8,128)} reduce(f32[16,1,124416]{2,1,0:T(1,128)} %all-to-all-done, f32[]{:T(128)} %constant.275), dimensions={1}, to_apply=%all_to_all.7.reduce_sub_computation | reduce | bytes 15925252 | tf_op jit(solution)/shard_map/all_to_all | solution.py:260
  530.8 6.3 reshape.2144
  537.1 9.3 %copy.56 = f32[4608,432]{1,0:T(8,128)} copy(f32[4608,432]{0,1:T(8,128)} %bitcast.232) | data formatting | bytes 15925248 | tf_op jit(solution)/shard_map/dot_general | solution.py:269
  546.3 14.7 %fusion.80 = f32[2,384,2,24,96]{1,4,3,2,0:T(8,128)S(1)} fusion(f32[2,24,96,432,1]{3,2,1,0,4:T(8,128)} %bitcast.231, f32[2,384,432,1,1]{1,0,2,4,3:T(2,128)S(1)} %bitcast.236), kind=kOutput, calls=%fused_computation.198 | convolution fusion | flops 9172942848 | bytes 23445504 | tf_op jit(solution)/shard_map/dot_general | solution.py:269
  561.0 3.2 fusion.77
  564.2 23.1 %fusion.55 = f32[2,16,27,2,24,96]{5,2,4,3,1,0:T(8,128)} fusion(f32[384,1,24,96]{0,3,2,1:T(8,128)S(1)} %get-tuple-element.268, f32[384,1,24,96]{0,3,2,1:T(8,128)S(1)} %get-tuple-element.267, f32[2,16,27,384,1,1]{3,2,1,0,4,5:T(8,128)S(1)} %reshape.2158), kind=kOutput, calls=%fused_computation.153 | convolution fusion | flops 9174712320 | bytes 24330240 | tf_op jit(solution)/shard_map/dot_general | solution.py:279
  587.3 6.2 fusion.58
  593.5 9.1 %fusion.60 = f32[16,27,24,1,96]{4,1,2,0,3:T(8,128)} fusion(f32[2,16,27,2,24,96]{5,2,4,3,1,0:T(8,128)} %fusion.55), kind=kLoop, calls=%fused_computation.163 | loop fusion | flops 995328 | bytes 11943936 | tf_op jit(solution)/shard_map/sub | solution.py:282
  602.6 9.4 %pad_maximum_fusion.2 = f32[16,27,24,2,96]{4,1,2,0,3:T(8,128)} fusion(f32[16,27,24,1,96]{4,1,2,0,3:T(8,128)S(1)} %fusion.58, f32[16,27,24,1,96]{4,1,2,0,3:T(8,128)} %fusion.60), kind=kLoop, calls=%fused_computation.148 | loop fusion | flops 1990656 | bytes 15925248 | tf_op jit(solution)/shard_map/stack | solution.py:281
  612.0 20.0 %copy.60 = f32[16,27,24,2,96]{4,3,2,1,0:T(2,128)} copy(f32[16,27,24,2,96]{4,1,2,0,3:T(8,128)} %pad_maximum_fusion.2) | data formatting | bytes 15925248
  632.0 96.8 %while.13 = (s32[]{:T(128)}, f32[16,3,256]{2,1,0:T(4,128)S(1)}, f32[16,27,24,2,96]{4,3,2,1,0:T(2,128)}, s32[16,3,256]{2,1,0:T(4,128)S(1)}, f32[16,3,256]{2,1,0:T...) while((s32[]{:T(128)}, f32[16,3,256]{2,1,0:T(4,128)S(1)}, ...), condition=%wide.region_12.13_spmd.clone, body=%wide.region_3.12_spmd.clone.sunk | while | flops 768924544 | bytes 11141737 | solution.py:292
  728.9 2.0 copy.69
  730.9 134.2 %reduce-scatter.4.cloned.1.call-done = f32[128,3]{1,0:T(8,128)} async-done(((f32[4096,3]{1,0:T(8,128)}), f32[128,3]{1,0:T(8,128)}) %reduce-scatter.4.cloned.1.call-update) | async-done | bytes 1552
  (492 shorter events, 105.0 us)
Async XLA Ops:
  21.9 20.1 %copy-start.1 = (s32[2,16]{1,0:T(2,128)}, s32[2,16]{1,0:T(2,128)S(1)}, u32[]{:S(2)}) copy-start(s32[2,16]{1,0:T(2,128)S(1)} %get-tuple-element.274.first_ref) | copy-start | bytes 388
  168.9 290.3 %all-to-all-start = ((f32[16,1,124416]{2,1,0:T(1,128)}), f32[16,1,124416]{2,1,0:T(1,128)}, u32[]{:S(2)}, u32[]{:S(2)}) async-start(f32[16,1,124416]{2,1,0:T(1,128)} %all_to_all.8), calls=%async_computation | async-start | bytes 15925248 | tf_op jit(solution)/shard_map/all_to_all | solution.py:260
  174.8 690.3 %reduce-scatter.4.cloned.1.call-start = ((), (), s32[]{:S(2)}) async-start(), calls=%async_computation.2 | async-start | bytes 2162688
  177.9 4.8 copy-start.2
  177.9 189.1 %copy-start.3 = (f32[3,128]{1,0:T(4,128)S(1)}, f32[3,128]{1,0:T(4,128)}, u32[]{:S(2)}) copy-start(f32[3,128]{1,0:T(4,128)} %param.10) | copy-start | bytes 4612
  537.1 9.3 %copy-start = (f32[2,384,432]{1,0,2:T(2,128)S(1)}, f32[2,384,432]{1,0,2:T(2,128)}, u32[]{:S(2)}) copy-start(f32[2,384,432]{1,0,2:T(2,128)} %dot_general.30) | copy-start | bytes 3981316
  728.9 2.0 copy-start.4
Sparse Core Ops, SparseCore 0:
  731.0 134.0 reduce-scatter.3
